TPU v7x, 512 devices: a whole 4x4x16 slice. The times are simulated.
512 devices in a mesh: dp: 32 (over y, x, core), tensor: 16 (over z).
Axes of the slice: x: 4, y: 4, z: 16, core: 2. Of those that a mesh axis runs over, the one named last changes fastest.
Arguments:
- tokens: bfloat16 [16384, 8192], P('dp', 'tensor'), may hold values from -6 to 6
- row_adapter_index: int32 [16384, 1], P('dp'), may hold values from 0 to 255; in each aligned block of 512 rows (0 to 511, 512 to 1023, ...) at most 4 rows name the same one
- adapter_storage_slot: int32 [256], replicated, may hold values from 0 to 255, each once
- key_value_base_weight: bfloat16 [8192, 2, 1024], P('tensor'), may hold values from -0.09375 to 0.09375
- adapter_down_weight: bfloat16 [256, 8192, 128], P('dp', 'tensor'), may hold values from -0.0625 to 0.0625
- adapter_up_weight: bfloat16 [256, 2, 64, 1024], P('dp', None, None, 'tensor'), may hold values from -0.75 to 0.75
Outputs:
- key_value: bfloat16 [16384, 2, 1024], P('dp', None, 'tensor')
Inputs may be any that keep to these rules, and one draw needn't show every extreme that they name: `row_adapter_index`: within the rows of one index of dp no adapter is named by more than 4 rows, a bound that some block reaches. `adapter_storage_slot`: A permutation of the slots.
All inputs are finite; a program needn't handle non-finite values.
Results may differ from a plain program's by a relative error of at most 0.0034.
Values may be sent and summed in bfloat16 or wider, within the bound.
A program may use at most 64 MiB of HBM per device.

v0:
```python
import jax
import jax.numpy as jnp
from jax import lax
from jax.sharding import PartitionSpec as P

adapter_scale = 0.5


def per_device(
    tokens,
    row_adapter_index,
    adapter_storage_slot,
    key_value_base_weight,
    adapter_down_weight,
    adapter_up_weight,
):
    row_count, shard_width = tokens.shape
    local_adapter_slots = adapter_down_weight.shape[0]
    groups = lax.axis_size("dp")
    experts = local_adapter_slots * groups
    capacity = max(2, 2 * row_count // experts)
    doubled_rank = adapter_down_weight.shape[2]
    adapter_of = row_adapter_index[:, 0]
    columns = lax.broadcasted_iota(jnp.int32, (row_count, experts), 1)
    onehot = (adapter_of[:, None] == columns).astype(jnp.int32)
    earlier = jnp.cumsum(onehot, axis=0) - onehot
    position = jnp.sum(earlier * onehot, axis=1)
    storage_device = jnp.sum(onehot * adapter_storage_slot[None, :], axis=1)
    target = storage_device * capacity + position
    outbox = jnp.zeros((experts * capacity, shard_width), tokens.dtype).at[target].set(tokens)
    outbox = outbox.reshape(groups, local_adapter_slots, capacity, shard_width)
    partials = jnp.einsum(
        "rd,djn->rjn", tokens, key_value_base_weight, preferred_element_type=jnp.float32
    )
    base = lax.psum_scatter(partials, "tensor", scatter_dimension=2, tiled=True)
    pieces_sum = jnp.einsum(
        "sekd,edr->sekr",
        lax.all_to_all(outbox, "dp", split_axis=0, concat_axis=0, tiled=True),
        adapter_down_weight,
        preferred_element_type=jnp.float32,
    )
    reduced_rows = lax.psum(pieces_sum, "tensor").astype(jnp.bfloat16)
    dims_now = reduced_rows.shape
    reduced_rows = reduced_rows.reshape(dims_now[0], dims_now[1], dims_now[2], 2, doubled_rank // 2)
    adapter_delta = jnp.einsum(
        "upgtl,ptlz->upgtz", reduced_rows, adapter_up_weight, preferred_element_type=jnp.float32
    )
    adapter_delta = (adapter_scale * adapter_delta).astype(jnp.bfloat16)
    returned = lax.all_to_all(adapter_delta, "dp", split_axis=0, concat_axis=0, tiled=True)
    returned_flat = returned.reshape(experts * capacity, 2, returned.shape[-1])
    update_rows = returned_flat[target]
    return (base + update_rows.astype(jnp.float32)).astype(jnp.bfloat16)


def solution(mesh):
    placed = (
        P("dp", "tensor"),
        P("dp", None),
        P(),
        P("tensor", None, None),
        P("dp", "tensor", None),
        P("dp", None, None, "tensor"),
    )
    return jax.shard_map(
        per_device, mesh=mesh, in_specs=placed, out_specs=P("dp", None, "tensor"), check_vma=False
    )
```

profile of v0, /device:TPU:1, one launch (start us, length us, event | category | flops | bytes accessed | tf_op | source)
XLA Modules:
  0.0 144.0 jit_solution(11326901580064575148)
XLA Ops:
  6.5 0.0 copy-start
  6.5 0.0 reduce-scatter.2.cloned.1.call-start
  6.5 1.6 %copy-done = bf16[512,2,1024]{2,1,0:T(2,128)(2,1)S(1)} copy-done((bf16[512,2,1024]{2,1,0:T(2,128)(2,1)S(1)}, bf16[512,2,1024]{2,1,0:T(2,128)(2,1)}, u32[]{:S(2)}) %copy-start) | copy-done | bytes 2097176
  8.1 4.3 %fusion = f32[512,2,1024]{0,2,1:T(8,128)} fusion(bf16[512,2,1024]{2,1,0:T(2,128)(2,1)S(1)} %copy-done, bf16[512,512]{1,0:T(8,128)(2,1)} %param.6), kind=kOutput, calls=%fused_computation.2 | convolution fusion | flops 1073741824 | bytes 6815744 | tf_op jit(solution)/shard_map/rd,djn->rjn/dot_general | solution.py:32
  12.4 0.0 copy-start.2
  12.4 0.0 reduce-scatter.2.cloned.1.call-update
  12.5 0.0 copy-start.3
  12.5 0.6 copy-done.2
  13.1 0.1 copy.19
  13.2 0.2 fusion.10
  13.5 0.1 copy.20
  13.6 0.0 copy-done.3
  13.7 0.4 select_reduce_fusion
  14.0 3.2 %scatter_custom_fusion = bf16[1024,512]{1,0:T(8,128)(2,1)S(1)} fusion(s32[512]{0:T(512)S(1)} %bitcast.51, bf16[512,512]{1,0:T(8,128)(2,1)} %param.6, bf16[]{:T(256)} %constant.5.clone.1), kind=kCustom, calls=%fused_computation.20 | custom fusion | bytes 1049088 | tf_op jit(solution)/shard_map/scatter | solution.py:30
  17.3 1.1 reshape.51
  18.4 0.0 copy-start.1
  18.4 27.9 %all_to_all.10 = bf16[32,8,4,512]{3,2,1,0:T(4,128)(2,1)S(1)} all-to-all(bf16[32,8,4,512]{3,2,1,0:T(4,128)(2,1)} %reshape.51), channel_id=1, replica_groups=mesh['dp'=32,'tensor'=16] {'dp'}, dimensions={0} | all-to-all | bytes 2097152 | tf_op jit(solution)/shard_map/all_to_all | solution.py:38
  46.3 0.0 copy-done.1
  46.3 0.0 copy-start.4
  46.3 0.8 convolution_bitcast_fusion
  47.1 61.2 %all-reduce.1 = bf16[32,8,4,128]{3,0,2,1:T(8,128)(2,1)S(1)} all-reduce(f32[32,8,4,128]{3,0,2,1:T(8,128)S(1)} %convolution_bitcast_fusion), channel_id=1, replica_groups=mesh['dp'=32,'tensor'=16] {'tensor'}, use_global_device_ids=true, to_apply=%region_6.7 | all-reduce | flops 131072 | bytes 786432 | tf_op jit(solution)/shard_map/psum | solution.py:42
  108.3 0.2 reshape.52
  108.5 0.0 copy-done.4
  108.5 0.3 fusion.3
  108.8 0.3 copy.36
  109.1 1.1 reshape.75
  110.2 13.0 %all-to-all-start.1 = ((bf16[32,2,2048]{2,1,0:T(2,128)(2,1)}), bf16[32,2,2048]{2,1,0:T(2,128)(2,1)S(1)}, u32[]{:S(2)}, u32[]{:S(2)}) async-start(bf16[32,2,2048]{2,1,0:T(2,128)(2,1)} %reshape.75), calls=%async_computation.2 | async-start | bytes 524288 | tf_op jit(solution)/shard_map/all_to_all | solution.py:49
  123.3 8.9 %all-to-all-done.1 = bf16[32,2,2048]{2,1,0:T(2,128)(2,1)S(1)} async-done(((bf16[32,2,2048]{2,1,0:T(2,128)(2,1)}), bf16[32,2,2048]{2,1,0:T(2,128)(2,1)S(1)}, u32[]{:S(2)}, u32[]{:S(2)}) %all-to-all-start.1) | async-done | bytes 262176 | tf_op jit(solution)/shard_map/all_to_all | solution.py:49
  132.1 0.4 reshape.76
  132.5 0.2 copy.24
  132.7 0.5 copy.25
  133.2 2.1 %gather_fusion = bf16[512,2,64]{2,1,0:T(2,128)(2,1)S(1)} fusion(bf16[1024,2,64]{2,1,0:T(2,128)(2,1)S(1)} %copy.25, s32[1024]{0:T(1024)S(1)} %pad_clamp_fusion), kind=kCustom, calls=%fused_computation | custom fusion | bytes 264192 | tf_op jit(solution)/shard_map/gather | solution.py:51
  135.4 0.1 copy.26
  135.5 0.0 reduce-scatter.2.cloned.1.call-done
  135.5 1.6 %add_convert_fusion = bf16[512,2,64]{0,2,1:T(8,128)(2,1)} fusion(f32[512,2,64]{0,2,1:T(8,128)} %reduce-scatter.2.cloned.1.call-done, bf16[512,2,64]{0,2,1:T(8,128)(2,1)S(1)} %copy.26), kind=kLoop, calls=%fused_computation.23 | loop fusion | flops 196608 | bytes 524288 | tf_op jit(solution)/shard_map/convert_element_type | solution.py:52
  (8 shorter events, 0.1 us)
Async XLA Ops:
  6.5 1.6 %copy-start = (bf16[512,2,1024]{2,1,0:T(2,128)(2,1)S(1)}, bf16[512,2,1024]{2,1,0:T(2,128)(2,1)}, u32[]{:S(2)}) copy-start(bf16[512,2,1024]{2,1,0:T(2,128)(2,1)} %param.9) | copy-start | bytes 6291460
  6.5 129.0 %reduce-scatter.2.cloned.1.call-start = ((), (), s32[]{:S(2)}) async-start(), calls=%async_computation.3 | async-start | bytes 4456448 | tf_op jit(solution)/shard_map/reduce_scatter | solution.py:35
  12.4 0.7 copy-start.2
  12.5 1.2 copy-start.3
  18.4 27.9 %copy-start.1 = (bf16[8,512,128]{2,1,0:T(8,128)(2,1)S(1)}, bf16[8,512,128]{2,1,0:T(8,128)(2,1)}, u32[]{:S(2)}) copy-start(bf16[8,512,128]{2,1,0:T(8,128)(2,1)} %param.10) | copy-start | bytes 3145732
  46.3 62.3 %copy-start.4 = (bf16[8,2,64,64]{3,2,1,0:T(8,128)(2,1)S(1)}, bf16[8,2,64,64]{3,2,1,0:T(8,128)(2,1)}, u32[]{:S(2)}) copy-start(bf16[8,2,64,64]{3,2,1,0:T(8,128)(2,1)} %param.11) | copy-start | bytes 393220
  110.2 22.0 %all-to-all-start.1 = ((bf16[32,2,2048]{2,1,0:T(2,128)(2,1)}), bf16[32,2,2048]{2,1,0:T(2,128)(2,1)S(1)}, u32[]{:S(2)}, u32[]{:S(2)}) async-start(bf16[32,2,2048]{2,1,0:T(2,128)(2,1)} %reshape.75), calls=%async_computation.2 | async-start | bytes 524288 | tf_op jit(solution)/shard_map/all_to_all | solution.py:49
Sparse Core Ops, SparseCore 0:
  12.6 79.6 reduce-scatter.1
where the time goes:
time: 144 us
  blocking collectives  89.1 us (62%)
  between operations  13.6 us (9%)
  starting transfers between devices  13 us (9%)
  local copies, waits for them, and re-layouts  11.8 us (8%)
  waiting for transfers between devices  8.92 us (6%)
  matrix products  5.38 us (4%)
  other arithmetic  2.28 us (2%)
    psum x1, blocking collectives, per_device(): reduced_rows = lax.psum(pieces_sum, 'tensor').astype(jnp.bfloat16)  61.2 us
    all_to_all x1, blocking collectives, per_device(): lax.all_to_all(outbox, 'dp', split_axis=0, concat_axis=0, tiled=True)  27.9 us
    all_to_all x1, starting transfers between devices, per_device(): lax.all_to_all(adapter_delta, 'dp', split_axis=0, concat_axis=0, tiled=True)  13 us
    all_to_all x1, waiting for transfers between devices, per_device(): lax.all_to_all(adapter_delta, 'dp', split_axis=0, concat_axis=0, tiled=True)  8.89 us
    dot_general x1, matrix products, per_device(): jnp.einsum('rd,djn->rjn', tokens, key_value_base_weight, preferred_elemen...  4.31 us
    unnamed x13, local copies, waits for them, and re-layouts  3.69 us
    scatter x1, local copies, waits for them, and re-layouts, per_device(): jnp.zeros((experts * capacity, shard_width), tokens.dtype).at[target]  3.22 us
  transfers between devices with their start and end apart: 2, of which 1 were waited for; matrix products, arithmetic and copies ran while one was open for 8% of the time, Pallas kernels for 0%

commit v1 on v0

v1 whole, which is shorter than its diff:
```python
import functools

import jax
import jax.numpy as jnp
from jax import lax
from jax.experimental import pallas as pl
from jax.experimental.pallas import tpu as pltpu
from jax.sharding import PartitionSpec as P

MESH = pl.DeviceIdType.MESH
BF = jnp.bfloat16
F32 = jnp.float32
I32 = jnp.int32
I16 = jnp.int16

Z = 16
SIDE = 4
DP = 32
ROWS = 512
SLOTS = 8
CAP = 4
PAIR = SLOTS * CAP
CHUNK = 2 * PAIR
Q = 4
QR = ROWS // Q
QX = QR + 16
LEVELS = 32000.0
SCALE = 0.5

PLAN = (
    ("S", 0), ("B", 0), ("L", 0), ("L", 1), ("B", 1), ("L", 2), ("L", 3), ("B", 2), ("L", 4), ("L", 5),
    ("B", 3), ("L", 6), ("L", 7), ("B", 4), ("LF", 0), ("G", 0), ("B", 5), ("GR", 0), ("U", 1), ("U", 2),
    ("U", 3), ("U", 4), ("B", 6), ("U", 5), ("U", 6), ("U", 7), ("U", 8), ("B", 7), ("BF", 0), ("H", 0),
)
REACH = 4
PAIRS = ((8, -7), (7, -6), (6, -5), (5, -3), (3, -2), (2, -1), (1, 0), (4, -4))


def kernel(
    x_hbm, idx_hbm, slot_hbm, w_hbm, down_hbm, up_hbm, out_ref,
    x_ref, idx_ref, slot_ref, w_ref, up_ref,
    perm, outbox, inbox, downcat, upbig, updates, returned, gath,
    b_send_r, b_send_l, b_recv_r, b_recv_l, own, base_t,
    l_send, l_recv, l_own,
    sem_in, sem_down, sem_br, sem_bl, sem_l, sem_g, sem_a, sem_ret,
    sent_br, sent_bl, sent_l, sent_g, sent_a, sent_ret,
):
    me = lax.axis_index("dp")
    z = lax.axis_index("tensor")
    core = lax.rem(me, 2)
    chip = me // 2
    y, x = chip // SIDE, lax.rem(chip, SIDE)
    right, left = lax.rem(z + 1, Z), lax.rem(z + Z - 1, Z)

    def mod_z(v):
        return lax.rem(v + 2 * Z, Z)

    def chip_at(q, sign):
        qy, qx = q // SIDE, lax.rem(q, SIDE)
        return lax.rem(y + sign * qy + SIDE, SIDE) * SIDE + lax.rem(x + sign * qx + SIDE, SIDE)

    def remote(src, dst, sent, got, dp, zz):
        return pltpu.make_async_remote_copy(
            src_ref=src, dst_ref=dst, send_sem=sent, recv_sem=got,
            device_id=(dp, zz), device_id_type=MESH,
        )

    barrier = pltpu.get_barrier_semaphore()

    @pl.loop(1, DP)
    def _(i):
        pl.semaphore_signal(
            barrier, inc=1, device_id=(lax.rem(me + i, DP), z), device_id_type=MESH
        )

    for k in range(1, REACH + 1):
        for zz in (mod_z(z + k), mod_z(z - k)):
            pl.semaphore_signal(barrier, inc=1, device_id=(me, zz), device_id_type=MESH)

    fetch = [
        pltpu.make_async_copy(src, dst, sem_in.at[i])
        for i, (src, dst) in enumerate(
            ((idx_hbm, idx_ref), (slot_hbm, slot_ref), (x_hbm, x_ref), (w_hbm, w_ref), (up_hbm, up_ref))
        )
    ]
    fetch_down = [
        pltpu.make_async_copy(down_hbm.at[e], downcat.at[:, e * 128:(e + 1) * 128], sem_down.at[e])
        for e in range(SLOTS)
    ]
    for copy in fetch + fetch_down:
        copy.start()

    fetch[0].wait()
    fetch[1].wait()
    adapters = idx_ref[...]
    names = slot_ref.shape[1]
    onehot = (lax.broadcasted_iota(I32, (names, ROWS), 0) == adapters).astype(F32).astype(BF)
    before = (
        lax.broadcasted_iota(I32, (ROWS, ROWS), 0) < lax.broadcasted_iota(I32, (ROWS, ROWS), 1)
    ).astype(F32).astype(BF)
    earlier = jnp.dot(onehot, before, preferred_element_type=F32)
    position = jnp.sum(earlier * onehot.astype(F32), axis=0, keepdims=True)
    slots = jnp.broadcast_to(slot_ref[...].astype(F32), (8, names)).astype(BF)
    storage = jnp.dot(slots, onehot, preferred_element_type=F32)[0:1, :]
    target = (storage * CAP + position).astype(I32)
    fetch[2].wait()
    tokens = x_ref[...]
    blk = 256
    for i in range(DP * PAIR // blk):
        part = (lax.broadcasted_iota(I32, (blk, ROWS), 0) + i * blk == target).astype(F32).astype(BF)
        perm[i * blk:(i + 1) * blk, :] = part
        outbox[i * blk:(i + 1) * blk, :] = jnp.dot(part, tokens, preferred_element_type=F32).astype(BF)

    def weight_of(c):
        tile = pl.ds(pl.multiple_of((c // 2) * 128, 128), 128)
        k, v = w_ref[:, 0, tile], w_ref[:, 1, tile]
        low = jnp.concatenate([k[:, :64], v[:, :64]], axis=1)
        high = jnp.concatenate([k[:, 64:], v[:, 64:]], axis=1)
        odd = jnp.broadcast_to(lax.rem(c, 2), low.shape) == 1
        return jnp.where(odd, high, low)

    def partial_of(c):
        return jnp.dot(x_ref[...], weight_of(c), preferred_element_type=F32)

    def encode(v, ref):
        top = jnp.max(jnp.abs(v), axis=0, keepdims=True)
        power = jnp.ceil(jnp.log(top + 1e-30) * 1.4426950408889634)
        code = jnp.round(v * (jnp.exp2(-power) * LEVELS))
        ref[0:QR, :] = code.astype(I32).astype(I16)
        ref[QR:QX, :] = jnp.broadcast_to(power, (16, 128)).astype(I32).astype(I16)

    def decode(ref):
        power = ref[QR:QX, :].astype(I32).astype(F32)[0:1, :]
        return ref[0:QR, :].astype(I32).astype(F32) * (jnp.exp2(power) * (1.0 / LEVELS))

    def base_step(s, send=True):
        part = partial_of(mod_z(z + 8 - s)) if send != "only" else None
        for b in range(Q):
            if send != "only":
                v = part[b * QR:(b + 1) * QR, :]
                if s > 0:
                    remote(b_send_r.at[s - 1, b], b_recv_r.at[s - 1, b], sent_br, sem_br.at[s - 1, b], me, right).wait_recv()
                    v = v + decode(b_recv_r.at[s - 1, b])
                encode(v, b_send_r.at[s, b])
            if send:
                remote(b_send_r.at[s, b], b_recv_r.at[s, b], sent_br, sem_br.at[s, b], me, right).start()
        part = partial_of(mod_z(z + 9 + s)) if send != "only" else None
        if s == 7:
            own[...] = part
            return
        for b in range(Q):
            if send != "only":
                v = part[b * QR:(b + 1) * QR, :]
                if s > 0:
                    remote(b_send_l.at[s - 1, b], b_recv_l.at[s - 1, b], sent_bl, sem_bl.at[s - 1, b], me, left).wait_recv()
                    v = v + decode(b_recv_l.at[s - 1, b])
                encode(v, b_send_l.at[s, b])
            if send:
                remote(b_send_l.at[s, b], b_recv_l.at[s, b], sent_bl, sem_bl.at[s, b], me, left).start()

    def base_final():
        for b in range(Q):
            remote(b_send_r.at[7, b], b_recv_r.at[7, b], sent_br, sem_br.at[7, b], me, right).wait_recv()
            remote(b_send_l.at[6, b], b_recv_l.at[6, b], sent_bl, sem_bl.at[6, b], me, left).wait_recv()
            rows = slice(b * QR, (b + 1) * QR)
            total = own[rows, :] + decode(b_recv_r.at[7, b]) + decode(b_recv_l.at[6, b])
            base_t[:, rows] = total.T

    def send_tokens():
        for k in range(Z):
            q = mod_z(z + PAIRS[k // 2][k % 2])
            there = chip_at(q, -1)
            mine = pl.ds(pl.multiple_of(q * CHUNK + core * PAIR, PAIR), PAIR)
            got = sem_a.at[q * 2 + core]
            for c in range(2):
                d = there * 2 + c
                src = outbox.at[pl.ds(pl.multiple_of(d * PAIR, PAIR), PAIR), :]

                @pl.when(d != me)
                def _():
                    remote(src, inbox.at[mine, :], sent_a, got, d, z).start()

                @pl.when(d == me)
                def _():
                    pltpu.make_async_copy(src, inbox.at[mine, :], got).start()

    def wait_tokens(q):
        for c in range(2):
            mine = inbox.at[pl.ds(pl.multiple_of(q * CHUNK + c * PAIR, PAIR), PAIR), :]
            pltpu.make_async_copy(mine, mine, sem_a.at[q * 2 + c]).wait()

    def chunk_rows(q):
        return pl.ds(pl.multiple_of(q * CHUNK, CHUNK), CHUNK)

    def adapter_of(rows):
        return lax.rem(lax.broadcasted_iota(I32, (rows, 128), 0), PAIR) // CAP

    def lora_send(i, dp_z, slot):
        return remote(l_send.at[i], l_recv.at[slot], sent_l, sem_l.at[slot], me, dp_z)

    def lora_step(s):
        offsets = PAIRS[s]
        chunks = [mod_z(z + o) for o in offsets]
        for q in chunks:
            wait_tokens(q)
        if s == 0:
            for copy in fetch_down:
                copy.wait()
        rows = jnp.concatenate([inbox[chunk_rows(q), :] for q in chunks], axis=0)
        full = jnp.dot(rows, downcat[...], preferred_element_type=F32)
        which = adapter_of(2 * CHUNK)
        piece = jnp.zeros((2 * CHUNK, 128), F32)
        for e in range(SLOTS):
            piece = jnp.where(which == e, full[:, e * 128:(e + 1) * 128], piece)
        for k, o in enumerate(offsets):
            mine = piece[k * CHUNK:(k + 1) * CHUNK, :]
            i = 2 * s + k
            far, sign = abs(o), (1 if o > 0 else -1)
            if o == 0:
                l_own[...] = mine
                continue
            if far > REACH:
                to, slot = sign * (far - REACH), (8 if o > 0 else 12) + far - REACH - 1
            else:
                to, slot = o, (0 if o > 0 else 4) + far - 1
            if far == REACH:
                for j in range(4 if o > 0 else 3):
                    got = (8 if o > 0 else 12) + j
                    lora_send(i, mod_z(z - sign * (j + 1)), got).wait_recv()
                    mine = mine + l_recv[got].astype(F32)
            l_send[i] = mine.astype(BF)
            lora_send(i, mod_z(z + to), slot).start()

    def lora_final():
        total = l_own[...]
        for slot in range(8):
            lora_send(0, mod_z(z + 1), slot).wait_recv()
            total = total + l_recv[slot].astype(F32)
        gath[z] = total.astype(BF)

    def gather_send(c, to, got):
        return remote(gath.at[c], gath.at[c], sent_g, sem_g.at[got], me, mod_z(z + to))

    def gather_wait(k):
        c = mod_z(z + k)
        gather_send(c, 1, (-k - 1) if k < 0 else 7 + k).wait_recv()

    def gather_first():
        for k in (4, 3, 2, 1):
            gather_send(z, k, k - 1).start()
            gather_send(z, -k, 7 + k).start()
        update_of([0])

    def gather_relay():
        gather_wait(-REACH)
        for k in (4, 3, 2, 1):
            gather_send(mod_z(z - REACH), k, k + REACH - 1).start()
        gather_wait(REACH)
        for k in (3, 2, 1):
            gather_send(mod_z(z + REACH), -k, 7 + k + REACH).start()

    def give_back(c):
        who = chip_at(c, 1)
        to = returned.at[pl.ds(pl.multiple_of(me * PAIR, PAIR), PAIR), :]
        for k in range(2):
            d = who * 2 + k
            src = updates.at[c, k * PAIR:(k + 1) * PAIR, :]

            @pl.when(d != me)
            def _():
                remote(src, to, sent_ret, sem_ret.at[me], d, z).start()

            @pl.when(d == me)
            def _():
                pltpu.make_async_copy(src, to, sem_ret.at[me]).start()

    def gather_step(k):
        offsets = [-k, k] if k < 8 else [-8]
        for o in offsets:
            if abs(o) != REACH:
                gather_wait(o)
        update_of(offsets)

    def update_of(offsets):
        chunks = [mod_z(z + o) for o in offsets]
        shrunk = [gath[c] for c in chunks]
        shrunk = jnp.concatenate(shrunk, axis=0) if len(chunks) > 1 else shrunk[0]
        which = adapter_of(CHUNK * len(chunks))
        spread = jnp.concatenate(
            [jnp.where(which == e, shrunk.astype(F32), 0.0).astype(BF) for e in range(SLOTS)], axis=1
        )
        delta = (SCALE * jnp.dot(spread, upbig[...], preferred_element_type=F32)).astype(BF)
        for i, c in enumerate(chunks):
            updates[c] = delta[i * CHUNK:(i + 1) * CHUNK, :]
            give_back(c)

    def finish():
        @pl.loop(0, DP)
        def _(i):
            part = returned.at[pl.ds(pl.multiple_of(i * PAIR, PAIR), PAIR), :]
            pltpu.make_async_copy(part, part, sem_ret.at[i]).wait()

        update_t = lax.dot_general(
            returned[...], perm[...], (((0,), (0,)), ((), ())), preferred_element_type=F32
        )
        out_ref[...] = (base_t[...] + update_t).astype(BF)

    def prepare():
        fetch[4].wait()
        for e in range(SLOTS):
            nothing = jnp.zeros((64, 64), BF)
            upbig[e * 128:e * 128 + 64, :] = jnp.concatenate([up_ref[e, 0], nothing], axis=1)
            upbig[e * 128 + 64:(e + 1) * 128, :] = jnp.concatenate([nothing, up_ref[e, 1]], axis=1)

    fetch[3].wait()
    base_step(0, False)
    pl.semaphore_wait(barrier, DP - 1 + 2 * REACH)
    for name, step in PLAN:
        if name == "S":
            send_tokens()
            prepare()
        elif name == "BF":
            base_final()
        elif name == "LF":
            lora_final()
        elif name == "H":
            finish()
        elif name == "B":
            base_step(step, True if step else "only")
        elif name == "L":
            lora_step(step)
        elif name == "G":
            gather_first()
        elif name == "GR":
            gather_relay()
        else:
            gather_step(step)

    def drain(ref, sem):
        pltpu.make_async_copy(ref, ref, sem).wait()

    drain(b_send_r, sent_br)
    drain(b_send_l, sent_bl)
    drain(l_send.at[0:15], sent_l)
    drain(gath.at[0:15], sent_g)
    drain(inbox.at[0:(DP - 1) * PAIR, :], sent_a)
    drain(returned.at[0:(DP - 1) * PAIR, :], sent_ret)


def per_device(tokens, row_adapter_index, storage_slot, base_weight, down, up):
    vmem = pl.BlockSpec(memory_space=pltpu.VMEM)
    dma = pltpu.SemaphoreType.DMA
    out = pl.pallas_call(
        kernel,
        out_shape=jax.ShapeDtypeStruct((128, ROWS), BF),
        in_specs=[pl.BlockSpec(memory_space=pltpu.HBM)] * 6,
        out_specs=vmem,
        scratch_shapes=[
            pltpu.VMEM((ROWS, 512), BF),
            pltpu.VMEM((1, ROWS), I32),
            pltpu.VMEM((1, storage_slot.shape[0]), I32),
            pltpu.VMEM(base_weight.shape, BF),
            pltpu.VMEM(up.shape, BF),
            pltpu.VMEM((DP * PAIR, ROWS), BF),
            pltpu.VMEM((DP * PAIR, 512), BF),
            pltpu.VMEM((DP * PAIR, 512), BF),
            pltpu.VMEM((512, SLOTS * 128), BF),
            pltpu.VMEM((SLOTS * 128, 128), BF),
            pltpu.VMEM((Z, CHUNK, 128), BF),
            pltpu.VMEM((DP * PAIR, 128), BF),
            pltpu.VMEM((Z, CHUNK, 128), BF),
            pltpu.VMEM((8, Q, QX, 128), I16),
            pltpu.VMEM((7, Q, QX, 128), I16),
            pltpu.VMEM((8, Q, QX, 128), I16),
            pltpu.VMEM((7, Q, QX, 128), I16),
            pltpu.VMEM((ROWS, 128), F32),
            pltpu.VMEM((128, ROWS), F32),
            pltpu.VMEM((Z, CHUNK, 128), BF),
            pltpu.VMEM((15, CHUNK, 128), BF),
            pltpu.VMEM((CHUNK, 128), F32),
            dma((5,)), dma((SLOTS,)), dma((8, Q)), dma((7, Q)), dma((15,)), dma((15,)), dma((DP,)), dma((DP,)),
            dma, dma, dma, dma, dma, dma,
        ],
        compiler_params=pltpu.CompilerParams(
            collective_id=0, has_side_effects=True, vmem_limit_bytes=60 << 20
        ),
    )(
        tokens,
        row_adapter_index.reshape(1, ROWS),
        storage_slot.reshape(1, -1),
        base_weight,
        down,
        up,
    )
    return out.reshape(2, 64, ROWS).transpose(2, 0, 1)


def solution(mesh):
    placed = (
        P("dp", "tensor"),
        P("dp", None),
        P(),
        P("tensor", None, None),
        P("dp", "tensor", None),
        P("dp", None, None, "tensor"),
    )
    return jax.shard_map(
        per_device, mesh=mesh, in_specs=placed, out_specs=P("dp", None, "tensor"), check_vma=False
    )
```

time: 144 us -> 70.2 us (0.49)
  blocking collectives: 89.1 us -> 0 us
  Pallas kernels: 0 us -> 68.1 us
  between operations: 13.6 us -> 0.01 us
  starting transfers between devices: 13 us -> 0 us
  local copies, waits for them, and re-layouts: 11.8 us -> 1.57 us
  waiting for transfers between devices: 8.92 us -> 0 us
  matrix products: 5.38 us -> 0 us
  other arithmetic: 2.28 us -> 0 us
    pallas_call x0 -> x1, Pallas kernels: none -> 68.1 us  [per_device(): pl.pallas_call(kernel, out_shape=jax.ShapeDtypeStruct((128, ROWS), BF), i...]
    psum x1 -> x0, blocking collectives: 61.2 us -> none  [per_device(): reduced_rows = lax.psum(pieces_sum, 'tensor').astype(jnp.bfloat16)]
    all_to_all x1 -> x0, blocking collectives: 27.9 us -> none  [per_device(): lax.all_to_all(outbox, 'dp', split_axis=0, concat_axis=0, tiled=True)]
    all_to_all x1 -> x0, starting transfers between devices: 13 us -> none  [per_device(): lax.all_to_all(adapter_delta, 'dp', split_axis=0, concat_axis=0, tiled=True)]
    all_to_all x1 -> x0, waiting for transfers between devices: 8.89 us -> none  [per_device(): lax.all_to_all(adapter_delta, 'dp', split_axis=0, concat_axis=0, tiled=True)]
    dot_general x3 -> x0, matrix products: 5.38 us -> none  [the longest x1 4.31 us: per_device(): jnp.einsum('rd,djn->rjn', tokens, key_value_base_weight, preferred_elemen...]
    scatter x1 -> x0, local copies, waits for them, and re-layouts: 3.22 us -> none  [per_device(): jnp.zeros((experts * capacity, shard_width), tokens.dtype).at[target]]
    gather x2 -> x0, local copies, waits for them, and re-layouts: 2.26 us -> none  [per_device(): update_rows = returned_flat[target]]
  transfers between devices with their start and end apart: 2 -> 0, of which waited for: 1 -> 0; matrix products, arithmetic and copies ran while one was open for 8% -> 0% of each run, Pallas kernels for 0% -> 0%
where the time goes in v1:
time: 70.2 us; the launch traced here: 69.7 us
  Pallas kernels  68.1 us (97%)
  local copies, waits for them, and re-layouts  1.57 us (2%)
    pallas_call x1, Pallas kernels, per_device(): pl.pallas_call(kernel, out_shape=jax.ShapeDtypeStruct((128, ROWS), BF), i...  68.1 us
    unnamed x1, local copies, waits for them, and re-layouts  1.57 us

profile of v1, /device:TPU:1, one launch (start us, length us, event | category | flops | bytes accessed | tf_op | source)
XLA Modules:
  0.0 69.7 jit_solution(10543022042692515224)
XLA Ops:
  0.0 68.1 %shard_map.64 = bf16[128,512]{1,0:T(8,128)(2,1)} custom-call(bf16[512,512]{1,0:T(8,128)(2,1)} %x_hbm.1, s32[1,512]{1,0:T(1,128)} %bitcast.6, s32[1,256]{1,0:T(1,128)} %bitcast.7, bf16[512,2,1024]{2,1,0:T(2,128)(2,1)} %w_hbm.1, bf16[8,512,128]{2,1,0:T(8,128)(2,1)} %down_hbm.1, bf16[8,2,64,64]{3,2,1,0:T(8,128)(2,1)} %up_hbm.1), custom_call_target="tpu_custom_call" | custom-call | tf_op jit(solution)/shard_map/pallas_call | solution.py:353
  68.1 1.6 %copy.8 = bf16[512,2,64]{0,2,1:T(8,128)(2,1)} copy(bf16[512,2,64]{0,2,1:T(8,128)(2,1)} %bitcast.5) | data formatting | bytes 262144

commit v2 on v1

--- a/solution.py
+++ b/solution.py
@@ -23,24 +23,21 @@
 CHUNK = 2 * PAIR
 Q = 4
 QR = ROWS // Q
-QX = QR + 16
+HEAD = 16
 LEVELS = 32000.0
+FINE = 256.0
 SCALE = 0.5
 
-PLAN = (
-    ("S", 0), ("B", 0), ("L", 0), ("L", 1), ("B", 1), ("L", 2), ("L", 3), ("B", 2), ("L", 4), ("L", 5),
-    ("B", 3), ("L", 6), ("L", 7), ("B", 4), ("LF", 0), ("G", 0), ("B", 5), ("GR", 0), ("U", 1), ("U", 2),
-    ("U", 3), ("U", 4), ("B", 6), ("U", 5), ("U", 6), ("U", 7), ("U", 8), ("B", 7), ("BF", 0), ("H", 0),
-)
+PLAN = (('S', 0), ('S', 1), ('B', 0), ('S', 2), ('S', 3), ('L', 0), ('L', 1), ('B', 1), ('S', 4), ('S', 5), ('L', 2), ('L', 3), ('B', 2), ('S', 6), ('S', 7), ('L', 4), ('L', 5), ('B', 3), ('L', 6), ('L', 7), ('B', 4), ('LF', 0), ('G', 0), ('B', 5), ('GR', 0), ('U', 1), ('U', 2), ('U', 3), ('U', 4), ('B', 6), ('U', 5), ('U', 6), ('U', 7), ('U', 8), ('B', 7), ('BF', 0), ('H', 0))
 REACH = 4
-PAIRS = ((8, -7), (7, -6), (6, -5), (5, -3), (3, -2), (2, -1), (1, 0), (4, -4))
+PAIRS = ((8, -7), (7, -6), (6, -5), (5, -3), (3, -2), (4, -4), (2, -1), (1, 0))
 
 
 def kernel(
     x_hbm, idx_hbm, slot_hbm, w_hbm, down_hbm, up_hbm, out_ref,
-    x_ref, idx_ref, slot_ref, w_ref, up_ref,
+    x_ref, idx_ref, slot_ref, w_ref, up_ref, w_all,
     perm, outbox, inbox, downcat, upbig, updates, returned, gath,
-    b_send_r, b_send_l, b_recv_r, b_recv_l, own, base_t,
+    b_send_r, b_send_l, b_recv_r, b_recv_l, part_r, part_l, top_r, top_l, base_t,
     l_send, l_recv, l_own,
     sem_in, sem_down, sem_br, sem_bl, sem_l, sem_g, sem_a, sem_ret,
     sent_br, sent_bl, sent_l, sent_g, sent_a, sent_ret,
@@ -111,64 +108,83 @@
         perm[i * blk:(i + 1) * blk, :] = part
         outbox[i * blk:(i + 1) * blk, :] = jnp.dot(part, tokens, preferred_element_type=F32).astype(BF)
 
-    def weight_of(c):
-        tile = pl.ds(pl.multiple_of((c // 2) * 128, 128), 128)
-        k, v = w_ref[:, 0, tile], w_ref[:, 1, tile]
-        low = jnp.concatenate([k[:, :64], v[:, :64]], axis=1)
-        high = jnp.concatenate([k[:, 64:], v[:, 64:]], axis=1)
-        odd = jnp.broadcast_to(lax.rem(c, 2), low.shape) == 1
-        return jnp.where(odd, high, low)
-
-    def partial_of(c):
-        return jnp.dot(x_ref[...], weight_of(c), preferred_element_type=F32)
-
-    def encode(v, ref):
-        top = jnp.max(jnp.abs(v), axis=0, keepdims=True)
-        power = jnp.ceil(jnp.log(top + 1e-30) * 1.4426950408889634)
-        code = jnp.round(v * (jnp.exp2(-power) * LEVELS))
-        ref[0:QR, :] = code.astype(I32).astype(I16)
-        ref[QR:QX, :] = jnp.broadcast_to(power, (16, 128)).astype(I32).astype(I16)
-
-    def decode(ref):
-        power = ref[QR:QX, :].astype(I32).astype(F32)[0:1, :]
-        return ref[0:QR, :].astype(I32).astype(F32) * (jnp.exp2(power) * (1.0 / LEVELS))
+    def arrange_weights():
+        first = lax.broadcasted_iota(I32, (512, 128), 1) < 64
+        for m in range(Z // 2):
+            pair = w_ref[:, :, m * 128:(m + 1) * 128].astype(F32)
+            k, v = pair[:, 0, :], pair[:, 1, :]
+            w_all[2 * m] = jnp.where(first, k, pltpu.roll(v, 64, 1)).astype(BF)
+            w_all[2 * m + 1] = jnp.where(first, pltpu.roll(k, 64, 1), v).astype(BF)
+
+    rings = (
+        (b_send_r, b_recv_r, sent_br, sem_br, part_r, top_r, right, 8),
+        (b_send_l, b_recv_l, sent_bl, sem_bl, part_l, top_l, left, 7),
+    )
+
+    def base_products(s):
+        weights = jnp.concatenate([w_all[mod_z(z + 8 - s)], w_all[mod_z(z + 9 + s)]], axis=1)
+        both = jnp.dot(x_ref[...], weights, preferred_element_type=F32)
+        for i, ring in enumerate(rings):
+            part = both[:, i * 128:(i + 1) * 128]
+            ring[4][...] = part
+            ring[5][...] = jnp.broadcast_to(jnp.max(jnp.abs(part), axis=0, keepdims=True), (8, 128))
+
+    def block_rows(b):
+        return slice(HEAD + b * QR, HEAD + (b + 1) * QR)
+
+    def base_copy(ring, s, b):
+        send, recv, sent, got, _, _, to, _ = ring
+        rows = slice(0, HEAD + QR) if b == 0 else block_rows(b)
+        return remote(send.at[s, rows, :], recv.at[s, rows, :], sent, got.at[s, b], me, to)
+
+    def power_in(recv, s):
+        return recv[s, 0:HEAD, :].astype(I32).astype(F32)[0:1, :] * (1.0 / FINE)
 
     def base_step(s, send=True):
-        part = partial_of(mod_z(z + 8 - s)) if send != "only" else None
+        held = [None, None]
         for b in range(Q):
-            if send != "only":
-                v = part[b * QR:(b + 1) * QR, :]
-                if s > 0:
-                    remote(b_send_r.at[s - 1, b], b_recv_r.at[s - 1, b], sent_br, sem_br.at[s - 1, b], me, right).wait_recv()
-                    v = v + decode(b_recv_r.at[s - 1, b])
-                encode(v, b_send_r.at[s, b])
-            if send:
-                remote(b_send_r.at[s, b], b_recv_r.at[s, b], sent_br, sem_br.at[s, b], me, right).start()
-        part = partial_of(mod_z(z + 9 + s)) if send != "only" else None
-        if s == 7:
-            own[...] = part
-            return
+            for i, ring in enumerate(rings):
+                out, recv, _, _, part, top, _, steps = ring
+                if s >= steps:
+                    continue
+                if send != "only":
+                    if s > 0:
+                        base_copy(ring, s - 1, b).wait_recv()
+                    if b == 0:
+                        bound = top[0:1, :] + 1e-30
+                        if s > 0:
+                            before_scale = jnp.exp2(power_in(recv, s - 1))
+                            bound = bound + before_scale
+                        power = jnp.ceil(jnp.log(bound) * (FINE * 1.4426950408889634))
+                        out[s, 0:HEAD, :] = jnp.broadcast_to(power, (HEAD, 128)).astype(I32).astype(I16)
+                        scale = jnp.exp2(power * (-1.0 / FINE)) * LEVELS
+                        held[i] = (scale, before_scale * scale * (1.0 / LEVELS) if s > 0 else None)
+                    scale, ratio = held[i]
+                    v = part[b * QR:(b + 1) * QR, :] * scale
+                    if s > 0:
+                        v = v + recv[s - 1, block_rows(b), :].astype(I32).astype(F32) * ratio
+                    out[s, block_rows(b), :] = jnp.round(v).astype(I32).astype(I16)
+                if send:
+                    base_copy(ring, s, b).start()
+        if send and s < 7:
+            base_products(s + 1)
+
+    def base_final():
+        scales = [None, None]
         for b in range(Q):
-            if send != "only":
-                v = part[b * QR:(b + 1) * QR, :]
-                if s > 0:
-                    remote(b_send_l.at[s - 1, b], b_recv_l.at[s - 1, b], sent_bl, sem_bl.at[s - 1, b], me, left).wait_recv()
-                    v = v + decode(b_recv_l.at[s - 1, b])
-                encode(v, b_send_l.at[s, b])
-            if send:
-                remote(b_send_l.at[s, b], b_recv_l.at[s, b], sent_bl, sem_bl.at[s, b], me, left).start()
-
-    def base_final():
-        for b in range(Q):
-            remote(b_send_r.at[7, b], b_recv_r.at[7, b], sent_br, sem_br.at[7, b], me, right).wait_recv()
-            remote(b_send_l.at[6, b], b_recv_l.at[6, b], sent_bl, sem_bl.at[6, b], me, left).wait_recv()
             rows = slice(b * QR, (b + 1) * QR)
-            total = own[rows, :] + decode(b_recv_r.at[7, b]) + decode(b_recv_l.at[6, b])
+            total = part_l[rows, :]
+            for i, ring in enumerate(rings):
+                last = ring[7] - 1
+                base_copy(ring, last, b).wait_recv()
+                if b == 0:
+                    scales[i] = jnp.exp2(power_in(ring[1], last)) * (1.0 / LEVELS)
+                total = total + ring[1][last, block_rows(b), :].astype(I32).astype(F32) * scales[i]
             base_t[:, rows] = total.T
 
-    def send_tokens():
-        for k in range(Z):
-            q = mod_z(z + PAIRS[k // 2][k % 2])
+    def send_tokens(step):
+        for offset in PAIRS[step]:
+            q = mod_z(z + offset)
             there = chip_at(q, -1)
             mine = pl.ds(pl.multiple_of(q * CHUNK + core * PAIR, PAIR), PAIR)
             got = sem_a.at[q * 2 + core]
@@ -312,13 +328,12 @@
             upbig[e * 128:e * 128 + 64, :] = jnp.concatenate([up_ref[e, 0], nothing], axis=1)
             upbig[e * 128 + 64:(e + 1) * 128, :] = jnp.concatenate([nothing, up_ref[e, 1]], axis=1)
 
-    fetch[3].wait()
-    base_step(0, False)
     pl.semaphore_wait(barrier, DP - 1 + 2 * REACH)
     for name, step in PLAN:
         if name == "S":
-            send_tokens()
-            prepare()
+            send_tokens(step)
+            if step == 7:
+                prepare()
         elif name == "BF":
             base_final()
         elif name == "LF":
@@ -326,7 +341,11 @@
         elif name == "H":
             finish()
         elif name == "B":
-            base_step(step, True if step else "only")
+            if step == 0:
+                fetch[3].wait()
+                arrange_weights()
+                base_products(0)
+            base_step(step)
         elif name == "L":
             lora_step(step)
         elif name == "G":
@@ -361,6 +380,7 @@
             pltpu.VMEM((1, storage_slot.shape[0]), I32),
             pltpu.VMEM(base_weight.shape, BF),
             pltpu.VMEM(up.shape, BF),
+            pltpu.VMEM((Z, 512, 128), BF),
             pltpu.VMEM((DP * PAIR, ROWS), BF),
             pltpu.VMEM((DP * PAIR, 512), BF),
             pltpu.VMEM((DP * PAIR, 512), BF),
@@ -369,11 +389,14 @@
             pltpu.VMEM((Z, CHUNK, 128), BF),
             pltpu.VMEM((DP * PAIR, 128), BF),
             pltpu.VMEM((Z, CHUNK, 128), BF),
-            pltpu.VMEM((8, Q, QX, 128), I16),
-            pltpu.VMEM((7, Q, QX, 128), I16),
-            pltpu.VMEM((8, Q, QX, 128), I16),
-            pltpu.VMEM((7, Q, QX, 128), I16),
+            pltpu.VMEM((8, HEAD + ROWS, 128), I16),
+            pltpu.VMEM((7, HEAD + ROWS, 128), I16),
+            pltpu.VMEM((8, HEAD + ROWS, 128), I16),
+            pltpu.VMEM((7, HEAD + ROWS, 128), I16),
             pltpu.VMEM((ROWS, 128), F32),
+            pltpu.VMEM((ROWS, 128), F32),
+            pltpu.VMEM((8, 128), F32),
+            pltpu.VMEM((8, 128), F32),
             pltpu.VMEM((128, ROWS), F32),
             pltpu.VMEM((Z, CHUNK, 128), BF),
             pltpu.VMEM((15, CHUNK, 128), BF),

time: 70.2 us -> 65.1 us (0.927)
  Pallas kernels: 68.1 us -> 63.4 us
    pallas_call x1, Pallas kernels: 68.1 us -> 63.4 us  [per_device(): pl.pallas_call(kernel, out_shape=jax.ShapeDtypeStruct((128, ROWS), BF), i...]
where the time goes in v2:
time: 65.1 us; the launch traced here: 65 us
  Pallas kernels  63.4 us (97%)
  local copies, waits for them, and re-layouts  1.57 us (2%)
    pallas_call x1, Pallas kernels, per_device(): pl.pallas_call(kernel, out_shape=jax.ShapeDtypeStruct((128, ROWS), BF), i...  63.4 us
    unnamed x1, local copies, waits for them, and re-layouts  1.57 us

profile of v2, /device:TPU:1, one launch (start us, length us, event | category | flops | bytes accessed | tf_op | source)
XLA Modules:
  0.0 65.0 jit_solution(4597244448544634985)
XLA Ops:
  0.0 63.4 %shard_map.64 = bf16[128,512]{1,0:T(8,128)(2,1)} custom-call(bf16[512,512]{1,0:T(8,128)(2,1)} %x_hbm.1, s32[1,512]{1,0:T(1,128)} %bitcast.6, s32[1,256]{1,0:T(1,128)} %bitcast.7, bf16[512,2,1024]{2,1,0:T(2,128)(2,1)} %w_hbm.1, bf16[8,512,128]{2,1,0:T(8,128)(2,1)} %down_hbm.1, bf16[8,2,64,64]{3,2,1,0:T(8,128)(2,1)} %up_hbm.1), custom_call_target="tpu_custom_call" | custom-call | tf_op jit(solution)/shard_map/pallas_call | solution.py:372
  63.4 1.6 %copy.8 = bf16[512,2,64]{0,2,1:T(8,128)(2,1)} copy(bf16[512,2,64]{0,2,1:T(8,128)(2,1)} %bitcast.5) | data formatting | bytes 262144
